TPU v7x, 256 devices: a whole 4x4x8 slice. The times are simulated.
256 devices in a mesh: band: 64 (over x, z, core), lev: 4 (over y).
Axes of the slice: x: 4, y: 4, z: 8, core: 2. Of those that a mesh axis runs over, the one named last changes fastest.
Arguments:
- obs_vals: bfloat16 [4, 24, 262144], P('lev', None, 'band'), may hold values from -400 to 400
- obs_colat: bfloat16 [262144], P('band'), may hold values from -1 to 1
- obs_lon: int32 [262144], P('band'), may hold values from 0 to 2047
- band_list: int32 [64, 64, 128], P('band'), may hold values from 0 to 4095, as said below
- counts: int32 [64, 64], P('band'), may hold values from 0 to 128, as said below
- w_in: bfloat16 [96, 256], replicated, may hold values from -0.625 to 0.625
- b_in: float32 [256], replicated, may hold values from -3 to 3
- w_out: bfloat16 [256, 256], P(None, 'lev'), may hold values from -0.375 to 0.375
- b_out: float32 [256], P('lev'), may hold values from -3 to 3
Outputs:
- encoded: bfloat16 [256, 2048, 512], P('lev', 'band')
Inputs may be any that keep to these rules, and one draw needn't show every extreme that they name: For each device s and band b the first counts[s, b] entries of band_list[s, b] are indices (within device s) of observations in band b; over all b they name every observation of device s exactly once. Later entries are padding and name arbitrary observations. `counts`: each row sums to 4096. Some band receives 128 observations from every device.
All inputs are finite; a program needn't handle non-finite values.
Results may differ from a plain program's by a relative error of at most 0.0063.
Values may be sent and summed in bfloat16 or wider, within the bound.
A program may use at most 64 MiB of HBM per device.

v0:
```python
import math

import jax
import jax.numpy as jnp
from jax import lax
from jax.sharding import PartitionSpec as P

LAT_DEV = 8
LON_DEV = 32


norm_eps = 1e-05


def cheb_inverse(nodes):
    order_ids = jnp.arange(nodes, dtype=jnp.float32)[:, None]
    node_ids = jnp.arange(nodes, dtype=jnp.float32)[None, :]
    factor = jnp.where(order_ids == 0.0, 1.0, 2.0).astype(jnp.float32) / nodes
    return factor * jnp.cos(math.pi * order_ids * (node_ids + 0.5) / nodes)


def lat_weights(colat, nodes):
    angles = jnp.arccos(jnp.clip(colat, -1.0, 1.0))
    order_ids = jnp.arange(nodes, dtype=jnp.float32)
    cheb_terms = jnp.cos(order_ids[:, None] * angles[None, :])
    return jnp.dot(cheb_inverse(nodes).T, cheb_terms, precision=lax.Precision.HIGHEST)


def dct_table(length):
    mode_ids = jnp.arange(length, dtype=jnp.float32)[:, None]
    node_ids = jnp.arange(length, dtype=jnp.float32)[None, :]
    row_scale = jnp.where(mode_ids == 0.0, math.sqrt(1.0 / length), math.sqrt(2.0 / length)).astype(
        jnp.float32
    )
    return (row_scale * jnp.cos(math.pi * mode_ids * (node_ids + 0.5) / length)).astype(
        jnp.bfloat16
    )


def on_device(obs_vals, obs_colat, obs_lon, band_list, counts, w_in, b_in, w_out, b_out):
    band_count = lax.axis_size("band")
    capacity = band_list.shape[2]
    lat_nodes = LAT_DEV
    lon_local = LON_DEV
    lon_count = lon_local * band_count
    lat_total = lat_nodes * band_count
    channels = obs_vals.shape[1]
    feat_count = w_in.shape[0]
    picked = band_list[0].reshape(-1)
    live_slot = (jnp.arange(capacity, dtype=jnp.int32)[None, :] < counts[0][:, None]).reshape(-1)
    outgoing = jnp.where(
        live_slot[None, :], jnp.take(obs_vals[0], picked, axis=1), jnp.zeros((), jnp.bfloat16)
    )
    colat_out = jnp.take(obs_colat, picked)[None, :]
    lon_out = jnp.take(obs_lon, picked)[None, :]
    incoming, colat_in, lon_in = (
        lax.all_to_all(outgoing, "band", split_axis=1, concat_axis=1, tiled=True),
        lax.all_to_all(colat_out, "band", split_axis=1, concat_axis=1, tiled=True),
        lax.all_to_all(lon_out, "band", split_axis=1, concat_axis=1, tiled=True),
    )
    weights = lat_weights(colat_in[0].astype(jnp.float32), lat_nodes)
    weighted = (incoming.astype(jnp.float32)[:, None, :] * weights[None]).astype(jnp.bfloat16)
    weighted = weighted.reshape(channels * lat_nodes, -1)
    lon_ids = lon_in[0]
    row_count = weighted.shape[1]
    block_rows = math.gcd(row_count, 1024)
    columns = jnp.arange(lon_count, dtype=jnp.int32)

    def add_block(step_index, grid_sum):
        first_row = step_index * block_rows
        block_vals = lax.dynamic_slice_in_dim(weighted, first_row, block_rows, 1)
        block_lon = lax.dynamic_slice_in_dim(lon_ids, first_row, block_rows, 0)
        onehot = (block_lon[:, None] == columns[None, :]).astype(jnp.bfloat16)
        return grid_sum + jnp.dot(block_vals, onehot, preferred_element_type=jnp.float32)

    grid_sum = lax.fori_loop(
        0,
        row_count // block_rows,
        add_block,
        jnp.zeros((channels * lat_nodes, lon_count), jnp.float32),
    )
    grid_half = grid_sum.astype(jnp.bfloat16).reshape(channels, lat_nodes, lon_count)
    all_levels = lax.all_gather(grid_half, "lev", axis=0, tiled=True)
    received = lax.all_to_all(all_levels, "band", split_axis=2, concat_axis=2, tiled=True)
    items = received.shape[0]
    arranged = received.reshape(items, lat_nodes, band_count, lon_local)
    table = dct_table(lat_total).reshape(lat_total, band_count, lat_nodes)
    spectrum = jnp.einsum(
        "cjbm,kbj->cmk", arranged, table, preferred_element_type=jnp.float32
    ).astype(jnp.bfloat16)
    pre_act = jnp.einsum("fh,fmk->hmk", w_in, spectrum, preferred_element_type=jnp.float32)
    squared = spectrum.astype(jnp.float32)
    pre_act, sum_sq = (pre_act, jnp.sum(squared * squared, axis=0))
    inv_norm = lax.rsqrt(sum_sq * (1.0 / feat_count) + norm_eps)
    hidden = jax.nn.gelu(pre_act * inv_norm[None] + b_in[:, None, None]).astype(jnp.bfloat16)
    output = (
        jnp.einsum("ho,hmk->omk", w_out, hidden, preferred_element_type=jnp.float32)
        + b_out[:, None, None]
    )
    return output.astype(jnp.bfloat16)


def solution(mesh):
    in_specs = (
        P("lev", None, "band"),
        P("band"),
        P("band"),
        P("band", None, None),
        P("band", None),
        P(),
        P(),
        P(None, "lev"),
        P("lev"),
    )
    out_specs = P("lev", "band", None)
    return jax.shard_map(
        on_device, mesh=mesh, in_specs=in_specs, out_specs=out_specs, check_vma=False
    )
```

profile of v0, /device:TPU:32, one launch (start us, length us, event | category | flops | bytes accessed | tf_op | source)
XLA Modules:
  0.0 416.9 jit_solution(8596966610472597191)
XLA Ops:
  6.5 0.8 compare_select_fusion
  7.4 45.5 %gather_fusion.2 = s32[8192]{0:T(1024)S(1)} fusion(s32[4096]{0:T(1024)S(1)} %copy-done.1, s32[8192]{0:T(1024)S(1)} %broadcast_clamp_fusion), kind=kCustom, calls=%fused_computation.2 | custom fusion | bytes 98304 | tf_op jit(solution)/shard_map/jit(_take)/gather | solution.py:55
  53.0 0.6 bitcast_select_fusion
  53.6 50.7 %gather_fusion.1 = bf16[8192]{0:T(1024)(128)(2,1)S(1)} fusion(bf16[4096]{0:T(1024)(128)(2,1)S(1)} %copy-done.2, s32[8192]{0:T(1024)S(1)} %broadcast_clamp_fusion), kind=kCustom, calls=%fused_computation.1 | custom fusion | bytes 65536 | tf_op jit(solution)/shard_map/jit(_take)/gather | solution.py:54
  104.4 0.6 copy.55
  105.0 11.6 %all-to-all-start.1 = ((bf16[1,64,128]{2,0,1:T(2,128)(2,1)}), bf16[1,64,128]{2,0,1:T(2,128)(2,1)S(1)}, u32[]{:S(2)}, u32[]{:S(2)}) async-start(bf16[1,64,128]{2,0,1:T(2,128)(2,1)} %copy.55), calls=%async_computation.1 | async-start | bytes 65536 | tf_op jit(solution)/shard_map/all_to_all | solution.py:58
  117.1 24.0 %gather_fusion = bf16[8192,24]{1,0:T(8,128)(2,1)S(1)} fusion(bf16[24,4096]{0,1:T(8,128)(2,1)S(1)} %bitcast.52, s32[8192]{0:T(1024)S(1)} %broadcast_clamp_fusion), kind=kCustom, calls=%fused_computation | custom fusion | bytes 819200 | tf_op jit(solution)/shard_map/jit(_take)/gather | solution.py:52
  141.2 0.9 copy.53
  142.1 0.9 select_select_fusion
  143.0 10.3 %all-to-all-start = ((bf16[24,64,128]{2,0,1:T(8,128)(2,1)}), bf16[24,64,128]{2,0,1:T(8,128)(2,1)S(1)}, u32[]{:S(2)}, u32[]{:S(2)}) async-start(bf16[24,64,128]{2,0,1:T(8,128)(2,1)} %select_select_fusion), calls=%async_computation | async-start | bytes 786432 | tf_op jit(solution)/shard_map/all_to_all | solution.py:57
  153.5 1.2 fusion.29
  154.8 13.0 %all-to-all-done = bf16[24,64,128]{2,0,1:T(8,128)(2,1)S(1)} async-done(((bf16[24,64,128]{2,0,1:T(8,128)(2,1)}), bf16[24,64,128]{2,0,1:T(8,128)(2,1)S(1)}, u32[]{:S(2)}, u32[]{:S(2)}) %all-to-all-start) | async-done | bytes 393248 | tf_op jit(solution)/shard_map/all_to_all | solution.py:57
  167.8 6.4 %all-to-all-start.2 = ((s32[1,64,128]{2,0,1:T(1,128)}), s32[1,64,128]{2,0,1:T(1,128)S(1)}, u32[]{:S(2)}, u32[]{:S(2)}) async-start(s32[1,64,128]{2,0,1:T(1,128)} %bitcast.11), calls=%async_computation.2 | async-start | bytes 65536 | tf_op jit(solution)/shard_map/all_to_all | solution.py:59
  174.7 8.0 %all-to-all-done.2 = s32[1,64,128]{2,0,1:T(1,128)S(1)} async-done(((s32[1,64,128]{2,0,1:T(1,128)}), s32[1,64,128]{2,0,1:T(1,128)S(1)}, u32[]{:S(2)}, u32[]{:S(2)}) %all-to-all-start.2) | async-done | bytes 32800 | tf_op jit(solution)/shard_map/all_to_all | solution.py:59
  182.7 35.7 %while.14 = (s32[]{:T(128)}, f32[192,2048]{1,0:T(8,128)}, bf16[192,8192]{1,0:T(8,128)(2,1)S(1)}, s32[8192]{0:T(1024)S(1)}, s32[]{:T(128)}, /*index=5*/s32[]{:T(128)}, s32[]{:T(128)}, s32[]{:T(128)}) while((s32[]{:T(128)}, f32[192,2048]{1,0:T(8,128)}, bf16[192,8192]{1,0:T(8,128)(2,1)S(1)}, s32[8192]{0:T(1024)S(1)}, s32[]{:T(128)}, ...), condition=%wide.region_1.2_spmd.clone, body=%wide.region_0.1_spmd.clone.sunk | while | flops 808189952 | bytes 3551381 | solution.py:76
  182.7 3.2 fusion.57
  186.0 4.6 %fusion.57 = f32[192,2048]{1,0:T(8,128)} fusion(s32[1024]{0:T(1024)S(1)} %dynamic_slice.21, f32[192,2048]{1,0:T(8,128)} %get-tuple-element.167, pred[]{:T(512)S(6)} %compare.3, bf16[192,8192]{1,0:T(8,128)(2,1)S(1)} %get-tuple-element.176, s32[]{:T(128)S(6)} %select_n.102), kind=kOutput, calls=%fused_computation.7.clone.1 | convolution fusion | flops 808189952 | bytes 3543045 | tf_op jit(solution)/shard_map/while/body/eval_jaxpr/dot_general | solution.py:74
  190.6 4.6 %fusion.57 = f32[192,2048]{1,0:T(8,128)} fusion(s32[1024]{0:T(1024)S(1)} %dynamic_slice.21, f32[192,2048]{1,0:T(8,128)} %get-tuple-element.167, pred[]{:T(512)S(6)} %compare.3, bf16[192,8192]{1,0:T(8,128)(2,1)S(1)} %get-tuple-element.176, s32[]{:T(128)S(6)} %select_n.102), kind=kOutput, calls=%fused_computation.7.clone.1 | convolution fusion | flops 808189952 | bytes 3543045 | tf_op jit(solution)/shard_map/while/body/eval_jaxpr/dot_general | solution.py:74
  195.2 4.6 %fusion.57 = f32[192,2048]{1,0:T(8,128)} fusion(s32[1024]{0:T(1024)S(1)} %dynamic_slice.21, f32[192,2048]{1,0:T(8,128)} %get-tuple-element.167, pred[]{:T(512)S(6)} %compare.3, bf16[192,8192]{1,0:T(8,128)(2,1)S(1)} %get-tuple-element.176, s32[]{:T(128)S(6)} %select_n.102), kind=kOutput, calls=%fused_computation.7.clone.1 | convolution fusion | flops 808189952 | bytes 3543045 | tf_op jit(solution)/shard_map/while/body/eval_jaxpr/dot_general | solution.py:74
  199.9 4.6 %fusion.57 = f32[192,2048]{1,0:T(8,128)} fusion(s32[1024]{0:T(1024)S(1)} %dynamic_slice.21, f32[192,2048]{1,0:T(8,128)} %get-tuple-element.167, pred[]{:T(512)S(6)} %compare.3, bf16[192,8192]{1,0:T(8,128)(2,1)S(1)} %get-tuple-element.176, s32[]{:T(128)S(6)} %select_n.102), kind=kOutput, calls=%fused_computation.7.clone.1 | convolution fusion | flops 808189952 | bytes 3543045 | tf_op jit(solution)/shard_map/while/body/eval_jaxpr/dot_general | solution.py:74
  204.5 4.6 %fusion.57 = f32[192,2048]{1,0:T(8,128)} fusion(s32[1024]{0:T(1024)S(1)} %dynamic_slice.21, f32[192,2048]{1,0:T(8,128)} %get-tuple-element.167, pred[]{:T(512)S(6)} %compare.3, bf16[192,8192]{1,0:T(8,128)(2,1)S(1)} %get-tuple-element.176, s32[]{:T(128)S(6)} %select_n.102), kind=kOutput, calls=%fused_computation.7.clone.1 | convolution fusion | flops 808189952 | bytes 3543045 | tf_op jit(solution)/shard_map/while/body/eval_jaxpr/dot_general | solution.py:74
  209.1 4.6 %fusion.57 = f32[192,2048]{1,0:T(8,128)} fusion(s32[1024]{0:T(1024)S(1)} %dynamic_slice.21, f32[192,2048]{1,0:T(8,128)} %get-tuple-element.167, pred[]{:T(512)S(6)} %compare.3, bf16[192,8192]{1,0:T(8,128)(2,1)S(1)} %get-tuple-element.176, s32[]{:T(128)S(6)} %select_n.102), kind=kOutput, calls=%fused_computation.7.clone.1 | convolution fusion | flops 808189952 | bytes 3543045 | tf_op jit(solution)/shard_map/while/body/eval_jaxpr/dot_general | solution.py:74
  213.8 4.6 %fusion.57 = f32[192,2048]{1,0:T(8,128)} fusion(s32[1024]{0:T(1024)S(1)} %dynamic_slice.21, f32[192,2048]{1,0:T(8,128)} %get-tuple-element.167, pred[]{:T(512)S(6)} %compare.3, bf16[192,8192]{1,0:T(8,128)(2,1)S(1)} %get-tuple-element.176, s32[]{:T(128)S(6)} %select_n.102), kind=kOutput, calls=%fused_computation.7.clone.1 | convolution fusion | flops 808189952 | bytes 3543045 | tf_op jit(solution)/shard_map/while/body/eval_jaxpr/dot_general | solution.py:74
  218.4 2.4 convert_bitcast_fusion.1
  220.8 38.0 %all-gather.2.cloned.1.call-done = bf16[96,8,2048]{2,1,0:T(8,128)(2,1)} async-done(((bf16[24,8,2048]{2,1,0:T(8,128)(2,1)}), bf16[96,8,2048]{2,1,0:T(8,128)(2,1)}) %all-gather.2.cloned.1.call-update) | async-done | bytes 3145744 | tf_op jit(solution)/shard_map/all_gather | solution.py:83
  258.8 7.0 %copy.57 = bf16[96,8,2048]{0,1,2:T(8,128)(2,1)} copy(bf16[96,8,2048]{2,1,0:T(8,128)(2,1)} %all-gather.2.cloned.1.call-done) | data formatting | bytes 6291456 | tf_op jit(solution)/shard_map/all_gather | solution.py:83
  265.8 10.7 %all-to-all-start.3 = ((bf16[96,8,2048]{0,1,2:T(8,128)(2,1)}), bf16[96,8,2048]{0,1,2:T(8,128)(2,1)}, u32[]{:S(2)}, u32[]{:S(2)}) async-start(bf16[96,8,2048]{0,1,2:T(8,128)(2,1)} %copy.57), calls=%async_computation.3 | async-start | bytes 8388608 | tf_op jit(solution)/shard_map/all_to_all | solution.py:84
  276.5 93.7 %all-to-all-done.3 = bf16[96,8,2048]{0,1,2:T(8,128)(2,1)} async-done(((bf16[96,8,2048]{0,1,2:T(8,128)(2,1)}), bf16[96,8,2048]{0,1,2:T(8,128)(2,1)}, u32[]{:S(2)}, u32[]{:S(2)}) %all-to-all-start.3) | async-done | bytes 3145760 | tf_op jit(solution)/shard_map/all_to_all | solution.py:84
  370.2 13.4 %copy.59 = bf16[96,8,64,32]{2,3,1,0:T(8,128)(2,1)} copy(bf16[96,8,64,32]{0,1,3,2:T(8,128)(2,1)} %bitcast.14) | data formatting | bytes 6291456 | tf_op jit(solution)/shard_map/reshape | solution.py:86
  383.6 11.2 %multiply_reduce_fusion = (f32[32,512]{1,0:T(8,128)S(1)}, bf16[96,32,512]{2,1,0:T(8,128)(2,1)}) fusion(bf16[96,8,64,32]{2,3,1,0:T(8,128)(2,1)} %copy.59, f32[64,8]{0,1:T(8,128)S(1)} %add_add_fusion, f32[512]{0:T(512)S(1)} %get-tuple-element.131, f32[512]{0:T(512)S(1)} %get-tuple-element.132), kind=kOutput, calls=%fused_computation.20 | convolution fusion | flops 1617936384 | bytes 6363136 | tf_op jit(solution)/shard_map/cjbm,kbj->cmk/dot_general | solution.py:88
  394.8 12.7 %fusion.20 = bf16[64,32,512]{2,0,1:T(8,128)(2,1)S(1)} fusion(f32[64]{0:T(128)S(1)} %copy-done.8, f32[256]{0:T(256)S(1)} %copy-done.7, f32[32,512]{1,0:T(8,128)S(1)} %add_rsqrt_fusion, bf16[96,32,512]{2,1,0:T(8,128)(2,1)} %get-tuple-element.128, bf16[96,256]{1,0:T(8,128)(2,1)S(1)} %copy-done, bf16[256,64]{0,1:T(8,128)(2,1)S(1)} %copy-done.6), kind=kOutput, calls=%fused_computation.26 | convolution fusion | flops 1390411776 | bytes 5391616 | tf_op jit(solution)/shard_map/ho,hmk->omk/dot_general | solution.py:97
  407.5 2.5 copy.62
  (44 shorter events, 1.4 us)
Async XLA Ops:
  6.5 388.2 %copy-start = (bf16[96,256]{1,0:T(8,128)(2,1)S(1)}, bf16[96,256]{1,0:T(8,128)(2,1)}, u32[]{:S(2)}) copy-start(bf16[96,256]{1,0:T(8,128)(2,1)} %param.16) | copy-start | bytes 147460
  6.5 0.8 copy-start.1
  7.4 45.6 %copy-start.3 = (s32[1,64,128]{2,1,0:T(8,128)S(1)}, s32[1,64,128]{2,1,0:T(8,128)}, u32[]{:S(2)}) copy-start(s32[1,64,128]{2,1,0:T(8,128)} %param.14) | copy-start | bytes 98308
  52.9 0.7 copy-start.2
  53.6 63.0 %copy-start.4 = (bf16[1,24,4096]{2,1,0:T(8,128)(2,1)S(1)}, bf16[1,24,4096]{2,1,0:T(8,128)(2,1)}, u32[]{:S(2)}) copy-start(bf16[1,24,4096]{2,1,0:T(8,128)(2,1)} %param.11) | copy-start | bytes 589828
  104.4 37.7 %copy-start.5 = (s32[1,64]{1,0:T(1,128)S(1)}, s32[1,64]{1,0:T(1,128)}, u32[]{:S(2)}) copy-start(s32[1,64]{1,0:T(1,128)} %param.15) | copy-start | bytes 772
  105.0 38.0 %all-to-all-start.1 = ((bf16[1,64,128]{2,0,1:T(2,128)(2,1)}), bf16[1,64,128]{2,0,1:T(2,128)(2,1)S(1)}, u32[]{:S(2)}, u32[]{:S(2)}) async-start(bf16[1,64,128]{2,0,1:T(2,128)(2,1)} %copy.55), calls=%async_computation.1 | async-start | bytes 65536 | tf_op jit(solution)/shard_map/all_to_all | solution.py:58
  143.0 24.8 %all-to-all-start = ((bf16[24,64,128]{2,0,1:T(8,128)(2,1)}), bf16[24,64,128]{2,0,1:T(8,128)(2,1)S(1)}, u32[]{:S(2)}, u32[]{:S(2)}) async-start(bf16[24,64,128]{2,0,1:T(8,128)(2,1)} %select_select_fusion), calls=%async_computation | async-start | bytes 786432 | tf_op jit(solution)/shard_map/all_to_all | solution.py:57
  167.8 15.0 %all-to-all-start.2 = ((s32[1,64,128]{2,0,1:T(1,128)}), s32[1,64,128]{2,0,1:T(1,128)S(1)}, u32[]{:S(2)}, u32[]{:S(2)}) async-start(s32[1,64,128]{2,0,1:T(1,128)} %bitcast.11), calls=%async_computation.2 | async-start | bytes 65536 | tf_op jit(solution)/shard_map/all_to_all | solution.py:59
  174.2 84.7 %all-gather.2.cloned.1.call-start = ((), (), s32[]{:S(2)}) async-start(), calls=%async_computation.4 | async-start | bytes 3932160 | tf_op jit(solution)/shard_map/all_gather | solution.py:83
  265.8 104.4 %all-to-all-start.3 = ((bf16[96,8,2048]{0,1,2:T(8,128)(2,1)}), bf16[96,8,2048]{0,1,2:T(8,128)(2,1)}, u32[]{:S(2)}, u32[]{:S(2)}) async-start(bf16[96,8,2048]{0,1,2:T(8,128)(2,1)} %copy.57), calls=%async_computation.3 | async-start | bytes 8388608 | tf_op jit(solution)/shard_map/all_to_all | solution.py:84
  383.6 11.2 %copy-start.6 = (bf16[256,64]{0,1:T(8,128)(2,1)S(1)}, bf16[256,64]{0,1:T(8,128)(2,1)}, u32[]{:S(2)}) copy-start(bf16[256,64]{0,1:T(8,128)(2,1)} %param.18) | copy-start | bytes 98308
  383.6 11.2 %copy-start.7 = (f32[256]{0:T(256)S(1)}, f32[256]{0:T(256)}, u32[]{:S(2)}) copy-start(f32[256]{0:T(256)} %param.17) | copy-start | bytes 3076
  383.6 11.2 %copy-start.8 = (f32[64]{0:T(128)S(1)}, f32[64]{0:T(128)}, u32[]{:S(2)}) copy-start(f32[64]{0:T(128)} %param.19) | copy-start | bytes 772
Sparse Core Ops, SparseCore 0:
  221.0 37.8 all-gather.1
where the time goes:
time: 421 us; the launch traced here: 417 us
  waiting for transfers between devices  153 us (36%)
  local copies, waits for them, and re-layouts  145 us (34%)
  matrix products  60.8 us (14%)
  starting transfers between devices  39 us (9%)
  between operations  13.7 us (3%)
  other arithmetic  5.5 us (1%)
    all_to_all x1, waiting for transfers between devices, on_device(): lax.all_to_all(all_levels, 'band', split_axis=2, concat_axis=2, tiled=True)  93.7 us
    gather x1, local copies, waits for them, and re-layouts, on_device(): colat_out = jnp.take(obs_colat, picked)[None, :]  50.7 us
    gather x1, local copies, waits for them, and re-layouts, on_device(): lon_out = jnp.take(obs_lon, picked)[None, :]  45.5 us
    all_gather x1, waiting for transfers between devices, on_device(): all_levels = lax.all_gather(grid_half, 'lev', axis=0, tiled=True)  38 us
    dot_general x8, matrix products, add_block(): jnp.dot(block_vals, onehot, preferred_element_type=jnp.float32)  35.6 us
    gather x2, local copies, waits for them, and re-layouts, on_device(): jnp.take(obs_vals[0], picked, axis=1)  24.9 us
    reshape x1, local copies, waits for them, and re-layouts, on_device(): arranged = received.reshape(items, lat_nodes, band_count, lon_local)  13.4 us
    all_to_all x1, waiting for transfers between devices, on_device(): lax.all_to_all(outgoing, 'band', split_axis=1, concat_axis=1, tiled=True)  13 us
  transfers between devices with their start and end apart: 5, of which 4 were waited for; matrix products, arithmetic and copies ran while one was open for 7% of the time, Pallas kernels for 0%

commit v1 on v0

v1 whole, which is shorter than its diff:
```python
import functools
import math

import jax
import jax.numpy as jnp
import numpy as np
from jax import lax
from jax.experimental import pallas as pl
from jax.experimental.pallas import tpu as pltpu
from jax.sharding import PartitionSpec as P

LAT = 8
LON = 32
CH = 24
CAP = 128
AUX = 32
LANES = 256
GROUP = 8
STRIDE = 27
EPS = 1e-05
F32, BF16, I32 = jnp.float32, jnp.bfloat16, jnp.int32
MESH = pl.DeviceIdType.MESH


def cheb_inverse():
    order = np.arange(LAT, dtype=np.float64)[:, None]
    node = np.arange(LAT, dtype=np.float64)[None, :]
    factor = np.where(order == 0.0, 1.0, 2.0) / LAT
    return (factor * np.cos(math.pi * order * (node + 0.5) / LAT)).astype(np.float32)


def dct_columns(length):
    mode = np.arange(length, dtype=np.float64)[None, :]
    node = np.arange(length, dtype=np.float64)[:, None]
    scale = np.where(mode == 0.0, math.sqrt(1.0 / length), math.sqrt(2.0 / length))
    return (scale * np.cos(math.pi * mode * (node + 0.5) / length)).astype(np.float32)


def rows_of(value, rows):
    return jnp.broadcast_to(value, (rows, value.shape[1]))


def kernel(
    nb, ny,
    vals, colat, lon, bl, cnt, inv_tab, dct, w_in, b_in, w_out, b_out,
    out,
    table, s1, r1, pm, qm, acc, grid, r2, spec, w1, w2, stage,
    send1, recv1, send2, recv2, send3, recv_l, recv_r, recv_o,
):
    me = lax.axis_index("band")
    lev = lax.axis_index("lev")
    right = lax.rem(lev + 1, ny)
    left = lax.rem(lev + ny - 1, ny)
    opp = lax.rem(lev + 2, ny)
    half_cols = CH * LON // 2
    groups = nb // GROUP
    width = GROUP * CAP
    hid = b_in.shape[0]

    def peer(i):
        return lax.rem(me + i * STRIDE, nb)

    barrier = pltpu.get_barrier_semaphore()

    @pl.loop(1, nb)
    def _(i):
        pl.semaphore_signal(barrier, inc=1, device_id={"band": peer(i)}, device_id_type=MESH)

    for y in (left, right):
        pl.semaphore_signal(barrier, inc=1, device_id={"lev": y}, device_id_type=MESH)

    obs = vals.shape[1]
    pieces = obs // LANES
    lon_v = lon[...]
    row8 = lax.broadcasted_iota(I32, (8, obs), 0)
    aux = jnp.where(
        row8 == 0,
        rows_of(colat[...].astype(F32), 8),
        jnp.where(
            row8 == 1,
            rows_of((lon_v // LON).astype(F32), 8),
            jnp.where(row8 == 2, rows_of((lon_v % LON).astype(F32), 8), 0.0),
        ),
    ).astype(BF16)
    for h in range(pieces):
        table[h * AUX : h * AUX + CH, :] = vals[:, h * LANES : (h + 1) * LANES]
        table[h * AUX + CH : (h + 1) * AUX, :] = aux[:, h * LANES : (h + 1) * LANES]

    batch = 4
    lane = lax.broadcasted_iota(I32, (1, CAP), 1)
    sub = lax.broadcasted_iota(I32, (LANES, CAP), 0)

    def sort_batch(step):
        hots, his = [], []
        for u in range(batch):
            b = peer(step * batch + u)
            idx = bl[pl.ds(b, 1), :]
            live = lane < cnt[pl.ds(b, 1), :]
            his.append(jnp.where(live, idx // LANES, -1))
            hots.append(jnp.where(sub == rows_of(idx % LANES, LANES), 1.0, 0.0).astype(BF16))
        picked = jnp.dot(table[...], jnp.concatenate(hots, 1), preferred_element_type=F32)
        hi = rows_of(jnp.concatenate(his, 1), AUX)
        block = jnp.zeros((AUX, batch * CAP), F32)
        for h in range(pieces):
            block = jnp.where(hi == h, picked[h * AUX : (h + 1) * AUX], block)
        block = block.astype(BF16)
        for u in range(batch):
            s1[step * batch + u] = block[:, u * CAP : (u + 1) * CAP]

    def send_block(i):
        pltpu.make_async_remote_copy(
            src_ref=s1.at[i], dst_ref=r1.at[i],
            send_sem=send1, recv_sem=recv1.at[i // GROUP],
            device_id={"band": peer(i)}, device_id_type=MESH,
        ).start()

    early = nb // batch // 2

    @pl.loop(0, early)
    def _(step):
        sort_batch(step)

    pl.semaphore_wait(barrier, nb - 1 + 2)
    own1 = pltpu.make_async_copy(s1.at[0], r1.at[0], recv1.at[0])
    own1.start()

    @pl.loop(1, early * batch)
    def _(i):
        send_block(i)

    @pl.loop(early, nb // batch)
    def _(step):
        sort_batch(step)
        for u in range(batch):
            send_block(step * batch + u)

    zero = jnp.zeros((CH, hid), F32)
    stacked = []
    for l in range(ny):
        w_l = w_in[l * CH : (l + 1) * CH, :].astype(F32)
        stacked.append(jnp.concatenate([w_l, zero], 1))
        stacked.append(jnp.concatenate([zero, w_l], 1))
    w1[...] = jnp.concatenate(stacked, 0).T.astype(BF16)
    w2[...] = (0.5 * w_out[...].astype(F32)).T.astype(BF16)

    odd8 = (lax.broadcasted_iota(I32, (2 * LAT, CAP), 0) // LAT).astype(F32)
    odd24 = (lax.broadcasted_iota(I32, (2 * CH, CAP), 0) // CH).astype(F32)
    nt = (((1,), (1,)), ((), ()))

    @pl.loop(0, groups)
    def _(g):
        pltpu.make_async_copy(
            s1.at[pl.ds(0, GROUP)], r1.at[pl.ds(0, GROUP)], recv1.at[g]
        ).wait()
        for t in range(GROUP):
            cols = slice(t * CAP, (t + 1) * CAP)
            got = r1[g * GROUP + t]
            tail = got[CH:AUX].astype(F32)
            x, hi, lo = tail[0:1], tail[1:2], tail[2:3]
            weight = rows_of(inv_tab[:, 0:1] * jnp.ones_like(x), LAT) + inv_tab[:, 1:2] * x
            t_prev, t_now = jnp.ones_like(x), x
            for k in range(2, LAT):
                t_prev, t_now = t_now, 2.0 * x * t_now - t_prev
                weight = weight + inv_tab[:, k : k + 1] * t_now
            w_two = jnp.concatenate([weight, weight], 0).astype(BF16)
            v_two = jnp.concatenate([got[0:CH].astype(F32)] * 2, 0).astype(BF16)
            hi_two = (rows_of(hi, 2 * LAT) - odd8).astype(BF16)
            lo_two = (rows_of(lo, 2 * CH) - odd24).astype(BF16)
            none8 = jnp.zeros((2 * LAT, CAP), BF16)
            none24 = jnp.zeros((2 * CH, CAP), BF16)
            for q in range(nb // 2):
                pm[g, q * 2 * LAT : (q + 1) * 2 * LAT, cols] = jnp.where(
                    hi_two == jnp.asarray(2.0 * q, BF16), w_two, none8
                )
            for q in range(LON // 2):
                qm[g, q * 2 * CH : (q + 1) * 2 * CH, cols] = jnp.where(
                    lo_two == jnp.asarray(2.0 * q, BF16), v_two, none24
                )
        part = lax.dot_general(pm[g], qm[g, 0:half_cols], nt, preferred_element_type=F32)

        @pl.when(g == 0)
        def _():
            acc[...] = part

        @pl.when(g > 0)
        def _():
            acc[...] += part

    def send_grid(h):
        grid[h] = acc[...].reshape(nb, LAT, half_cols).astype(BF16)
        pltpu.make_async_copy(grid.at[h, me], r2.at[h, me], recv2.at[h]).start()

        @pl.loop(1, nb)
        def _(i):
            to = peer(i)
            pltpu.make_async_remote_copy(
                src_ref=grid.at[h, to], dst_ref=r2.at[h, me],
                send_sem=send2.at[h], recv_sem=recv2.at[h],
                device_id={"band": to}, device_id_type=MESH,
            ).start()

    send_grid(0)

    @pl.loop(0, groups)
    def _(g):
        part = lax.dot_general(
            pm[g], qm[g, half_cols : 2 * half_cols], nt, preferred_element_type=F32
        )

        @pl.when(g == 0)
        def _():
            acc[...] = part

        @pl.when(g > 0)
        def _():
            acc[...] += part

    send_grid(1)

    def transform(h):
        pltpu.make_async_copy(grid.at[h], r2.at[h], recv2.at[h]).wait()
        nodes = r2[h].astype(F32).reshape(nb * LAT, half_cols).astype(BF16)
        modes = lax.dot_general(
            nodes, dct[...], (((0,), (0,)), ((), ())), preferred_element_type=F32
        )
        spec[lev, h * half_cols : (h + 1) * half_cols, :] = modes.astype(BF16)

    chunks = 8
    rows = CH * LON // chunks

    def piece(level, i):
        return spec.at[level, i * rows : (i + 1) * rows]

    def push(level, i, to, sem):
        pltpu.make_async_remote_copy(
            src_ref=piece(level, i), dst_ref=piece(level, i),
            send_sem=send3, recv_sem=sem.at[i],
            device_id={"lev": to}, device_id_type=MESH,
        ).start()

    def arrived(level, i, sem):
        pltpu.make_async_copy(piece(level, i), piece(level, i), sem.at[i]).wait()

    def own(i):
        push(lev, i, right, recv_l)
        push(lev, i, left, recv_r)

    def relay(i):
        arrived(left, i, recv_l)
        if i % 2 == 0:
            push(left, i, right, recv_o)
        arrived(right, i, recv_r)
        if i % 2 == 1:
            push(right, i, left, recv_o)

    def encode(i):
        arrived(opp, i, recv_o)
        pairs = rows // (2 * CH)
        for p in range(i * pairs, (i + 1) * pairs):
            feats = spec[:, p * 2 * CH : (p + 1) * 2 * CH, :]
            wide = feats.astype(F32)
            square = jnp.sum(wide * wide, axis=0)
            pre = jnp.dot(
                w1[...], feats.reshape(ny * 2 * CH, feats.shape[2]), preferred_element_type=F32
            )
            for par in range(2):
                mean = jnp.sum(square[par * CH : (par + 1) * CH], axis=0, keepdims=True)
                norm = lax.rsqrt(mean * (1.0 / (ny * CH)) + EPS)
                z = pre[par * hid : (par + 1) * hid] * norm + b_in[...]
                bend = jnp.tanh(z * (0.7978845608028654 + 0.035677408136300125 * (z * z)))
                hidden = (z + z * bend).astype(BF16)
                stage[:, 2 * p + par, :] = (
                    jnp.dot(w2[...], hidden, preferred_element_type=F32) + b_out[...]
                )
        done = LON // chunks
        if i % 2 == 1:
            lo_m, hi_m = (i - 1) * done, (i + 1) * done
            out[:, lo_m:hi_m, :] = stage[:, lo_m:hi_m, :].astype(BF16)

    half = chunks // 2
    transform(0)
    for i in range(half):
        own(i)
    for i in range(half):
        relay(i)
    transform(1)
    for i in range(half, chunks):
        own(i)
    for i in range(half):
        encode(i)
        relay(half + i)
    for i in range(half, chunks):
        encode(i)

    pltpu.make_async_copy(s1.at[pl.ds(0, nb - 1)], r1.at[pl.ds(0, nb - 1)], send1).wait()
    for h in range(2):
        sent = grid.at[h, pl.ds(0, nb - 1)]
        pltpu.make_async_copy(sent, sent, send2.at[h]).wait()
    sent = spec.at[pl.ds(0, 3)]
    pltpu.make_async_copy(sent, sent, send3).wait()


def on_device(nb, ny, obs_vals, obs_colat, obs_lon, band_list, counts, w_in, b_in, w_out, b_out):
    obs = obs_vals.shape[2]
    modes = nb * LAT
    outs = w_out.shape[1]
    half_cols = CH * LON // 2
    groups = nb // GROUP
    width = GROUP * CAP
    dma = pltpu.SemaphoreType.DMA
    vmem = pl.BlockSpec(memory_space=pltpu.VMEM)
    return pl.pallas_call(
        functools.partial(kernel, nb, ny),
        out_shape=jax.ShapeDtypeStruct((outs, LON, modes), BF16),
        in_specs=[vmem] * 11,
        out_specs=vmem,
        scratch_shapes=[
            pltpu.VMEM((obs // LANES * AUX, LANES), BF16),
            pltpu.VMEM((nb, AUX, CAP), BF16),
            pltpu.VMEM((nb, AUX, CAP), BF16),
            pltpu.VMEM((groups, nb * LAT, width), BF16),
            pltpu.VMEM((groups, LON * CH, width), BF16),
            pltpu.VMEM((nb * LAT, half_cols), F32),
            pltpu.VMEM((2, nb, LAT, half_cols), BF16),
            pltpu.VMEM((2, nb, LAT, half_cols), BF16),
            pltpu.VMEM((ny, LON * CH, modes), BF16),
            pltpu.VMEM((2 * w_in.shape[1], 2 * w_in.shape[0]), BF16),
            pltpu.VMEM((outs, w_out.shape[0]), BF16),
            pltpu.VMEM((outs, LON, modes), F32),
            dma, dma((groups,)), dma((2,)), dma((2,)), dma, dma((8,)), dma((8,)), dma((8,)),
        ],
        compiler_params=pltpu.CompilerParams(
            collective_id=0, has_side_effects=True, vmem_limit_bytes=62 * 1024 * 1024
        ),
    )(
        obs_vals[0],
        obs_colat[None, :],
        obs_lon[None, :],
        band_list[0],
        counts.reshape(nb, 1),
        jnp.asarray(cheb_inverse().T),
        jnp.asarray(dct_columns(modes)).astype(BF16),
        w_in,
        b_in[:, None],
        w_out,
        b_out[:, None],
    )


def solution(mesh):
    nb, ny = mesh.shape["band"], mesh.shape["lev"]
    in_specs = (
        P("lev", None, "band"),
        P("band"),
        P("band"),
        P("band", None, None),
        P("band", None),
        P(),
        P(),
        P(None, "lev"),
        P("lev"),
    )
    return jax.shard_map(
        functools.partial(on_device, nb, ny),
        mesh=mesh, in_specs=in_specs, out_specs=P("lev", "band", None), check_vma=False,
    )
```

time: 421 us -> 85.5 us (0.20)
  waiting for transfers between devices: 153 us -> 0 us
  local copies, waits for them, and re-layouts: 145 us -> 10.1 us
  Pallas kernels: 0 us -> 75.1 us
  matrix products: 60.8 us -> 0 us
  starting transfers between devices: 39 us -> 0 us
  between operations: 13.7 us -> 0.01 us
  other arithmetic: 5.5 us -> 0 us
    gather x4 -> x0, local copies, waits for them, and re-layouts: 121 us -> none  [the longest x1 50.7 us: on_device(): colat_out = jnp.take(obs_colat, picked)[None, :]]
    all_to_all x4 -> x0, waiting for transfers between devices: 115 us -> none  [the longest x1 93.7 us: on_device(): lax.all_to_all(all_levels, 'band', split_axis=2, concat_axis=2, tiled=True)]
    pallas_call x0 -> x1, Pallas kernels: none -> 75.1 us  [on_device(): pl.pallas_call(functools.partial(kernel, nb, ny), out_shape=jax.ShapeDtyp...]
    dot_general x11 -> x0, matrix products: 60.8 us -> none  [the longest x8 35.6 us: add_block(): jnp.dot(block_vals, onehot, preferred_element_type=jnp.float32)]
    all_to_all x4 -> x0, starting transfers between devices: 38.9 us -> none  [the longest x1 11.6 us: on_device(): lax.all_to_all(colat_out, 'band', split_axis=1, concat_axis=1, tiled=True)]
    all_gather x1 -> x0, waiting for transfers between devices: 38 us -> none  [on_device(): all_levels = lax.all_gather(grid_half, 'lev', axis=0, tiled=True)]
    reshape x1, local copies, waits for them, and re-layouts: 13.4 us -> 1.34 us  [on_device(): counts.reshape(nb, 1)]
    all_gather x1 -> x0, local copies, waits for them, and re-layouts: 7.01 us -> none  [on_device(): all_levels = lax.all_gather(grid_half, 'lev', axis=0, tiled=True)]
  transfers between devices with their start and end apart: 5 -> 0, of which waited for: 4 -> 0; matrix products, arithmetic and copies ran while one was open for 7% -> 0% of each run, Pallas kernels for 0% -> 0%
where the time goes in v1:
time: 85.5 us; the launch traced here: 85.2 us
  Pallas kernels  75.1 us (88%)
  local copies, waits for them, and re-layouts  10.1 us (12%)
    pallas_call x1, Pallas kernels, on_device(): pl.pallas_call(functools.partial(kernel, nb, ny), out_shape=jax.ShapeDtyp...  75.1 us
    unnamed x2, local copies, waits for them, and re-layouts  4.64 us

profile of v1, /device:TPU:32, one launch (start us, length us, event | category | flops | bytes accessed | tf_op | source)
XLA Modules:
  0.0 85.2 jit_solution(1122614556290109393)
XLA Ops:
  0.0 1.3 %broadcast_in_dim.12.colat = bf16[1,4096]{1,0:T(2,128)(2,1)} reshape(bf16[4096]{0:T(1024)(128)(2,1)} %param.12) | data formatting | bytes 16384 | tf_op jit(solution)/shard_map/broadcast_in_dim | solution.py:337
  1.3 1.3 %copy.15.cnt = s32[64,1]{1,0:T(8,128)} copy(s32[64,1]{0,1:T(1,128)} %bitcast.10) | data formatting | bytes 512 | tf_op jit(solution)/shard_map/reshape | solution.py:340
  2.6 1.3 %copy.18.b_out = f32[64,1]{1,0:T(8,128)} copy(f32[64,1]{0,1:T(1,128)} %bitcast.11) | data formatting | bytes 512 | tf_op jit(solution)/shard_map/broadcast_in_dim | solution.py:346
  4.0 1.5 %copy.17.w_out = bf16[256,64]{1,0:T(8,128)(2,1)} copy(bf16[256,64]{0,1:T(8,128)(2,1)} %param.18) | data formatting | bytes 65536 | tf_op args[7]
  5.5 1.5 %copy.16.b_in = f32[256,1]{1,0:T(8,128)} copy(f32[256,1]{0,1:T(1,128)} %bitcast.9) | data formatting | bytes 2048 | tf_op jit(solution)/shard_map/broadcast_in_dim | solution.py:344
  6.9 75.1 %shard_map.109 = bf16[64,32,512]{2,1,0:T(8,128)(2,1)} custom-call(bf16[24,4096]{1,0:T(8,128)(2,1)} %bitcast.6, bf16[1,4096]{1,0:T(2,128)(2,1)} %broadcast_in_dim.12.colat, s32[1,4096]{1,0:T(1,128)} %bitcast.8, s32[64,128]{1,0:T(8,128)} %bitcast.7, s32[64,1]{1,0:T(8,128)} %copy.15.cnt, f32[8,8]{1,0:T(8,128)} %constant.4.clone.inv_tab, ...), custom_call_target="tpu_custom_call" | custom-call | tf_op jit(solution)/shard_map/pallas_call | solution.py:312
  82.0 3.2 %copy.20 = bf16[64,32,512]{2,1,0:T(8,128)(2,1)} copy(bf16[64,32,512]{2,1,0:T(8,128)(2,1)} %shard_map.109) | data formatting | bytes 4194304

commit v2 on v1

v2 whole, which is shorter than its diff:
```python
import functools
import math

import jax
import jax.numpy as jnp
import numpy as np
from jax import lax
from jax.experimental import pallas as pl
from jax.experimental.pallas import tpu as pltpu
from jax.sharding import PartitionSpec as P

LAT = 8
LON = 32
CH = 24
CAP = 128
AUX = 32
LANES = 256
INPUTS = 11
GROUP = 8
STRIDE = 27
PARTS = 3
SPLIT = 2
DEPTH = 8
PIECES = 12
ROWS = 16
EPS = 1e-05
F32, BF16, I32 = jnp.float32, jnp.bfloat16, jnp.int32
MESH = pl.DeviceIdType.MESH


def cheb_inverse():
    order = np.arange(LAT, dtype=np.float64)[:, None]
    node = np.arange(LAT, dtype=np.float64)[None, :]
    factor = np.where(order == 0.0, 1.0, 2.0) / LAT
    return (factor * np.cos(math.pi * order * (node + 0.5) / LAT)).astype(np.float32)


def dct_columns(length):
    mode = np.arange(length, dtype=np.float64)[None, :]
    node = np.arange(length, dtype=np.float64)[:, None]
    scale = np.where(mode == 0.0, math.sqrt(1.0 / length), math.sqrt(2.0 / length))
    return (scale * np.cos(math.pi * mode * (node + 0.5) / length)).astype(np.float32)


def rows_of(value, rows):
    return jnp.broadcast_to(value, (rows, value.shape[1]))


def kernel(
    nb, ny,
    *refs,
):
    hbm, out, local = refs[:INPUTS], refs[INPUTS], refs[INPUTS + 1 : 2 * INPUTS + 1]
    vals, colat, lon, bl, cnt, inv_tab, dct, w_in, b_in, w_out, b_out = local
    (
        live_n, bias1, bias2, table, s1, r1, prep, acc, grid, r2, spec, w1, w2, pre, stage,
        load, send1, recv1, send2, recv2, send3, recv_l, recv_r, recv_o,
    ) = refs[2 * INPUTS + 1 :]
    me = lax.axis_index("band")
    lev = lax.axis_index("lev")
    right = lax.rem(lev + 1, ny)
    left = lax.rem(lev + ny - 1, ny)
    opp = lax.rem(lev + 2, ny)
    part_cols = CH * LON // PARTS
    send_cols = part_cols // SPLIT
    groups = nb // GROUP
    hid = b_in.shape[1]

    def peer(i):
        return lax.rem(me + i * STRIDE, nb)

    loads = [pltpu.make_async_copy(hbm[k], local[k], load.at[k]) for k in range(INPUTS)]
    for copy in loads:
        copy.start()
    barrier = pltpu.get_barrier_semaphore()

    @pl.loop(1, nb)
    def _(i):
        pl.semaphore_signal(barrier, inc=1, device_id={"band": peer(i)}, device_id_type=MESH)

    for y in (left, right):
        pl.semaphore_signal(barrier, inc=1, device_id={"lev": y}, device_id_type=MESH)

    for copy in loads:
        copy.wait()
    for row, column in ((cnt, live_n), (b_in, bias1), (b_out, bias2)):
        n, copies = row.shape[1], column.shape[1]
        r_id = lax.broadcasted_iota(I32, (n, n), 0)
        c_id = lax.broadcasted_iota(I32, (n, n), 1)
        wide_row = rows_of(row[...].astype(F32), n)
        one = jnp.sum(jnp.where(r_id == c_id, wide_row, 0.0), axis=1, keepdims=True)
        column[...] = jnp.broadcast_to(one, (n, copies))

    obs = vals.shape[1]
    pieces = obs // LANES
    lon_v = lon[...]
    lon_hi, lon_lo = (lon_v // LON).astype(F32), (lon_v % LON).astype(F32)
    pos = colat[...].astype(F32)
    row8 = lax.broadcasted_iota(I32, (8, CAP), 0)
    for h in range(pieces):
        table[h * AUX : h * AUX + CH, :] = vals[:, h * LANES : (h + 1) * LANES]
        for part in range(LANES // CAP):
            r = h * (LANES // CAP) + part
            aux = jnp.zeros((8, CAP), F32)
            for k, source in enumerate((pos, lon_hi, lon_lo)):
                aux = jnp.where(row8 == k, rows_of(source[r : r + 1], 8), aux)
            table[h * AUX + CH : (h + 1) * AUX, part * CAP : (part + 1) * CAP] = aux.astype(BF16)

    batch = 4
    lane = lax.broadcasted_iota(I32, (1, CAP), 1)
    sub = lax.broadcasted_iota(I32, (LANES, CAP), 0)

    def sort_batch(step):
        hots, his = [], []
        for u in range(batch):
            b = peer(step * batch + u)
            idx = bl[pl.ds(b, 1), :]
            live = lane.astype(F32) < live_n[pl.ds(b, 1), :]
            his.append(jnp.where(live, idx // LANES, -1))
            hots.append(jnp.where(sub == rows_of(idx % LANES, LANES), 1.0, 0.0).astype(BF16))
        picked = jnp.dot(table[...], jnp.concatenate(hots, 1), preferred_element_type=F32)
        hi = rows_of(jnp.concatenate(his, 1), AUX)
        block = jnp.zeros((AUX, batch * CAP), F32)
        for h in range(pieces):
            block = jnp.where(hi == h, picked[h * AUX : (h + 1) * AUX], block)
        block = block.astype(BF16)
        for u in range(batch):
            s1[step * batch + u] = block[:, u * CAP : (u + 1) * CAP]

    def send_block(i):
        pltpu.make_async_remote_copy(
            src_ref=s1.at[i], dst_ref=r1.at[i],
            send_sem=send1, recv_sem=recv1.at[i // GROUP],
            device_id={"band": peer(i)}, device_id_type=MESH,
        ).start()

    @pl.loop(0, nb // batch)
    def _(step):
        sort_batch(step)

    pl.semaphore_wait(barrier, nb - 1 + 2)
    pltpu.make_async_copy(s1.at[0], r1.at[0], recv1.at[0]).start()

    @pl.loop(1, nb)
    def _(i):
        send_block(i)

    zero = jnp.zeros((CH, hid), F32)
    stacked = []
    for l in range(ny):
        w_l = w_in[l * CH : (l + 1) * CH, :].astype(F32)
        stacked.append(jnp.concatenate([w_l, zero], 1))
        stacked.append(jnp.concatenate([zero, w_l], 1))
    w1[...] = jnp.concatenate(stacked, 0).T.astype(BF16)
    w2[...] = (0.5 * w_out[...].astype(F32)).astype(BF16)

    odd8 = (lax.broadcasted_iota(I32, (2 * LAT, CAP), 0) // LAT).astype(F32)
    odd24 = (lax.broadcasted_iota(I32, (2 * CH, CAP), 0) // CH).astype(F32)
    nt = (((1,), (1,)), ((), ()))

    def add_part(n, g):
        total = None
        for first in range(0, GROUP, DEPTH):
            lefts, rights = [], []
            for t in range(first, first + DEPTH):
                block = prep[g * GROUP + t].astype(BF16)
                hi_two, w_two = block[0 : 2 * LAT], block[2 * LAT : 4 * LAT]
                none = jnp.zeros_like(w_two)
                lefts.append(
                    jnp.concatenate(
                        [
                            jnp.where(hi_two == jnp.asarray(2.0 * q, BF16), w_two, none)
                            for q in range(nb // 2)
                        ]
                    )
                )
                tiles = []
                for tile in range(n * part_cols // 16, (n + 1) * part_cols // 16):
                    q, third = divmod(tile, 3)
                    at = 4 * LAT + 16 * third
                    tiles.append(
                        jnp.where(
                            block[at : at + 16] == jnp.asarray(2.0 * q, BF16),
                            block[at + 2 * CH : at + 2 * CH + 16],
                            none,
                        )
                    )
                rights.append(jnp.concatenate(tiles))
            term = lax.dot_general(
                jnp.concatenate(lefts, 1), jnp.concatenate(rights, 1), nt,
                preferred_element_type=F32,
            )
            total = term if total is None else total + term
        acc[...] += total

    clear = jnp.zeros(acc.shape, F32)
    columns = [jnp.broadcast_to(inv_tab[:, k : k + 1], (LAT, CAP)) for k in range(LAT)]
    acc[...] = clear

    @pl.loop(0, groups)
    def _(g):
        pltpu.make_async_copy(
            s1.at[pl.ds(0, GROUP)], r1.at[pl.ds(0, GROUP)], recv1.at[g]
        ).wait()
        for t in range(GROUP):
            got = r1[g * GROUP + t]
            tail = got[CH:AUX].astype(F32)
            x, hi, lo = tail[0:1], tail[1:2], tail[2:3]
            weight = columns[0] + columns[1] * x
            t_prev, t_now = jnp.ones_like(x), x
            for k in range(2, LAT):
                t_prev, t_now = t_now, 2.0 * x * t_now - t_prev
                weight = weight + columns[k] * t_now
            values = got[0:CH].astype(F32)
            prep[g * GROUP + t] = jnp.concatenate(
                [rows_of(hi, 2 * LAT) - odd8, weight, weight, rows_of(lo, 2 * CH) - odd24, values, values]
            )
        add_part(0, g)

    def send_grid(n):
        for s in range(n * SPLIT, (n + 1) * SPLIT):
            cols = slice((s - n * SPLIT) * send_cols, (s - n * SPLIT + 1) * send_cols)
            grid[s] = acc[:, cols].reshape(nb, LAT, send_cols).astype(BF16)
            pltpu.make_async_copy(grid.at[s, me], r2.at[s, me], recv2.at[s]).start()

            @pl.loop(1, nb)
            def _(i):
                to = peer(i)
                pltpu.make_async_remote_copy(
                    src_ref=grid.at[s, to], dst_ref=r2.at[s, me],
                    send_sem=send2.at[s], recv_sem=recv2.at[s],
                    device_id={"band": to}, device_id_type=MESH,
                ).start()

    send_grid(0)
    for n in range(1, PARTS):
        acc[...] = clear

        @pl.loop(0, groups)
        def _(g):
            add_part(n, g)

        send_grid(n)

    def transform(n):
        pltpu.make_async_copy(grid.at[n], r2.at[n], recv2.at[n]).wait()
        nodes = r2[n].astype(F32).reshape(nb * LAT, send_cols).astype(BF16)
        modes = lax.dot_general(
            nodes, dct[...], (((0,), (0,)), ((), ())), preferred_element_type=F32
        )
        spec[lev, n * send_cols : (n + 1) * send_cols, :] = modes.astype(BF16)

    rows = CH * LON // PIECES

    def piece(level, i):
        return spec.at[level, i * rows : (i + 1) * rows]

    def push(level, i, to, sem):
        pltpu.make_async_remote_copy(
            src_ref=piece(level, i), dst_ref=piece(level, i),
            send_sem=send3, recv_sem=sem.at[i],
            device_id={"lev": to}, device_id_type=MESH,
        ).start()

    def arrived(level, i, sem):
        pltpu.make_async_copy(piece(level, i), piece(level, i), sem.at[i]).wait()

    def own(i):
        push(lev, i, right, recv_l)
        push(lev, i, left, recv_r)

    def relay(i):
        if i % 2 == 0:
            arrived(left, i, recv_l)
            push(left, i, right, recv_o)
        else:
            arrived(right, i, recv_r)
            push(right, i, left, recv_o)

    def encode(p):
        first = pl.multiple_of(p * 2 * CH, 2 * CH)
        feats = spec[:, pl.ds(first, 2 * CH), :]
        modes = feats.shape[2]
        wide = feats.astype(F32)
        square = jnp.sum(wide * wide, axis=0)
        pre[...] = jnp.dot(
            w1[...], feats.reshape(ny * 2 * CH, modes), preferred_element_type=F32
        )
        for par in range(2):
            mean = jnp.sum(square[par * CH : (par + 1) * CH], axis=0, keepdims=True)
            norm = rows_of(lax.rsqrt(mean * (1.0 / (ny * CH)) + EPS), ROWS)
            act = []
            for r in range(0, hid, ROWS):
                bias = jnp.concatenate([bias1[r : r + ROWS, :]] * (modes // CAP), 1)
                z = pre[par * hid + r : par * hid + r + ROWS, :] * norm + bias
                bend = jnp.tanh(z * (0.7978845608028654 + 0.035677408136300125 * (z * z)))
                act.append((z + z * bend).astype(BF16))
            stage[:, 2 * p + par, :] = (
                jnp.dot(w2[...], jnp.concatenate(act), preferred_element_type=F32) + bias2[...]
            )

    ready = [(i + 1) * rows // (2 * CH) for i in range(PIECES)]

    def encode_piece(i):
        if i % 2 == 0:
            arrived(right, i, recv_r)
        else:
            arrived(left, i, recv_l)
        arrived(opp, i, recv_o)
        before = ready[i - 1] if i else 0

        @pl.loop(before, ready[i])
        def _(p):
            encode(p)

        lo_m, hi_m = before * 2 // 8 * 8, ready[i] * 2 // 8 * 8
        if hi_m > lo_m:
            out[:, lo_m:hi_m, :] = stage[:, lo_m:hi_m, :].astype(BF16)

    for n in range(PARTS * SPLIT):
        transform(n)
        own(2 * n)
        own(2 * n + 1)
        if n in (1, 2, 3):
            relay(2 * n - 2)
            relay(2 * n - 1)
    encode_piece(0)
    encode_piece(1)
    relay(6)
    relay(7)
    encode_piece(2)
    encode_piece(3)
    relay(8)
    relay(9)
    for i in range(4, 8):
        encode_piece(i)
    relay(10)
    relay(11)
    for i in range(8, PIECES):
        encode_piece(i)

    pltpu.make_async_copy(s1.at[pl.ds(0, nb - 1)], r1.at[pl.ds(0, nb - 1)], send1).wait()
    for h in range(PARTS * SPLIT):
        sent = grid.at[h, pl.ds(0, nb - 1)]
        pltpu.make_async_copy(sent, sent, send2.at[h]).wait()
    sent = spec.at[pl.ds(0, 3)]
    pltpu.make_async_copy(sent, sent, send3).wait()


def on_device(nb, ny, obs_vals, obs_colat, obs_lon, band_list, counts, w_in, b_in, w_out, b_out):
    obs = obs_vals.shape[2]
    modes = nb * LAT
    outs = w_out.shape[1]
    part_cols = CH * LON // PARTS
    send_cols = part_cols // SPLIT
    groups = nb // GROUP
    dma = pltpu.SemaphoreType.DMA
    vmem = pl.BlockSpec(memory_space=pltpu.VMEM)
    args = (
        obs_vals[0],
        obs_colat.reshape(obs // CAP, CAP),
        obs_lon.reshape(obs // CAP, CAP),
        band_list[0],
        counts,
        jnp.asarray(cheb_inverse().T),
        jnp.asarray(dct_columns(modes)).astype(BF16),
        w_in,
        b_in[None, :],
        w_out.T,
        b_out[None, :],
    )
    return pl.pallas_call(
        functools.partial(kernel, nb, ny),
        out_shape=jax.ShapeDtypeStruct((outs, LON, modes), BF16),
        in_specs=[pl.BlockSpec(memory_space=pltpu.HBM)] * INPUTS,
        out_specs=vmem,
        scratch_shapes=[
            *(pltpu.VMEM(arg.shape, arg.dtype) for arg in args),
            pltpu.VMEM((nb, 1), F32),
            pltpu.VMEM((w_in.shape[1], CAP), F32),
            pltpu.VMEM((outs, 1), F32),
            pltpu.VMEM((obs // LANES * AUX, LANES), BF16),
            pltpu.VMEM((nb, AUX, CAP), BF16),
            pltpu.VMEM((nb, AUX, CAP), BF16),
            pltpu.VMEM((nb, 4 * LAT + 4 * CH, CAP), F32),
            pltpu.VMEM((nb * LAT, part_cols), F32),
            pltpu.VMEM((PARTS * SPLIT, nb, LAT, send_cols), BF16),
            pltpu.VMEM((PARTS * SPLIT, nb, LAT, send_cols), BF16),
            pltpu.VMEM((ny, LON * CH, modes), BF16),
            pltpu.VMEM((2 * w_in.shape[1], 2 * w_in.shape[0]), BF16),
            pltpu.VMEM((outs, w_out.shape[0]), BF16),
            pltpu.VMEM((2 * w_in.shape[1], modes), F32),
            pltpu.VMEM((outs, LON, modes), F32),
            dma((INPUTS,)), dma, dma((groups,)), dma((PARTS * SPLIT,)), dma((PARTS * SPLIT,)),
            dma, dma((PIECES,)), dma((PIECES,)), dma((PIECES,)),
        ],
        compiler_params=pltpu.CompilerParams(
            collective_id=0, has_side_effects=True, vmem_limit_bytes=40 * 1024 * 1024
        ),
    )(*(pltpu.with_memory_space_constraint(arg, pltpu.HBM) for arg in args))


def solution(mesh):
    nb, ny = mesh.shape["band"], mesh.shape["lev"]
    in_specs = (
        P("lev", None, "band"),
        P("band"),
        P("band"),
        P("band", None, None),
        P("band", None),
        P(),
        P(),
        P(None, "lev"),
        P("lev"),
    )
    return jax.shard_map(
        functools.partial(on_device, nb, ny),
        mesh=mesh, in_specs=in_specs, out_specs=P("lev", "band", None), check_vma=False,
    )
```

time: 85.5 us -> 76.1 us (0.89)
  local copies, waits for them, and re-layouts: 10.1 us -> 1.32 us
  Pallas kernels: 75.1 us -> 74 us
    broadcast_in_dim x3 -> x0, local copies, waits for them, and re-layouts: 4.11 us -> none  [the longest x1 1.47 us: on_device(): b_in[:, None]]
    unnamed x2 -> x1, local copies, waits for them, and re-layouts: 4.64 us -> 1.32 us
    reshape x1 -> x0, local copies, waits for them, and re-layouts: 1.34 us -> none  [on_device(): counts.reshape(nb, 1)]
    pallas_call x1, Pallas kernels: 75.1 us -> 74 us  [on_device(): pl.pallas_call(functools.partial(kernel, nb, ny), out_shape=jax.ShapeDtyp...]
where the time goes in v2:
time: 76.1 us; the launch traced here: 75.3 us
  Pallas kernels  74 us (97%)
  local copies, waits for them, and re-layouts  1.32 us (2%)
    pallas_call x1, Pallas kernels, on_device(): pl.pallas_call(functools.partial(kernel, nb, ny), out_shape=jax.ShapeDtyp...  74 us

profile of v2, /device:TPU:32, one launch (start us, length us, event | category | flops | bytes accessed | tf_op | source)
XLA Modules:
  0.0 75.3 jit_solution(3241332722607403205)
XLA Ops:
  0.0 74.0 %shard_map.109 = bf16[64,32,512]{2,1,0:T(8,128)(2,1)S(1)} custom-call(bf16[24,4096]{1,0:T(8,128)(2,1)} %bitcast.7, bf16[32,128]{1,0:T(8,128)(2,1)} %bitcast.11, s32[32,128]{1,0:T(8,128)} %bitcast.10, s32[64,128]{1,0:T(8,128)} %bitcast.8, s32[1,64]{1,0:T(1,128)} %refs_4_.1, f32[8,8]{1,0:T(8,128)} %constant.4.clone.refs_5_, bf16[512,512]{1,0:T(8,128)(2,1)} %constant.9.refs_6_, ...), custom_call_target="tpu_custom_call" | custom-call | tf_op jit(solution)/shard_map/pallas_call | solution.py:372
  74.0 1.3 %copy.13 = bf16[64,32,512]{2,1,0:T(8,128)(2,1)} copy(bf16[64,32,512]{2,1,0:T(8,128)(2,1)S(1)} %shard_map.109) | data formatting | bytes 4194304

commit v3 on v2

--- a/solution.py
+++ b/solution.py
@@ -22,6 +22,7 @@
 SPLIT = 2
 DEPTH = 8
 PIECES = 12
+STRIPS = 1
 ROWS = 16
 EPS = 1e-05
 F32, BF16, I32 = jnp.float32, jnp.bfloat16, jnp.int32
@@ -53,7 +54,7 @@
     hbm, out, local = refs[:INPUTS], refs[INPUTS], refs[INPUTS + 1 : 2 * INPUTS + 1]
     vals, colat, lon, bl, cnt, inv_tab, dct, w_in, b_in, w_out, b_out = local
     (
-        live_n, bias1, bias2, table, s1, r1, prep, acc, grid, r2, spec, w1, w2, pre, stage,
+        live_n, bias2, table, s1, r1, prep, acc, grid, r2, spec, w1, w2, pre, stage,
         load, send1, recv1, send2, recv2, send3, recv_l, recv_r, recv_o,
     ) = refs[2 * INPUTS + 1 :]
     me = lax.axis_index("band")
@@ -83,7 +84,7 @@
 
     for copy in loads:
         copy.wait()
-    for row, column in ((cnt, live_n), (b_in, bias1), (b_out, bias2)):
+    for row, column in ((cnt, live_n), (b_out, bias2)):
         n, copies = row.shape[1], column.shape[1]
         r_id = lax.broadcasted_iota(I32, (n, n), 0)
         c_id = lax.broadcasted_iota(I32, (n, n), 1)
@@ -134,16 +135,24 @@
             device_id={"band": peer(i)}, device_id_type=MESH,
         ).start()
 
-    @pl.loop(0, nb // batch)
+    early = nb // batch * 3 // 4
+
+    @pl.loop(0, early)
     def _(step):
         sort_batch(step)
 
     pl.semaphore_wait(barrier, nb - 1 + 2)
     pltpu.make_async_copy(s1.at[0], r1.at[0], recv1.at[0]).start()
 
-    @pl.loop(1, nb)
+    @pl.loop(1, early * batch)
     def _(i):
         send_block(i)
+
+    @pl.loop(early, nb // batch)
+    def _(step):
+        sort_batch(step)
+        for u in range(batch):
+            send_block(step * batch + u)
 
     zero = jnp.zeros((CH, hid), F32)
     stacked = []
@@ -151,6 +160,12 @@
         w_l = w_in[l * CH : (l + 1) * CH, :].astype(F32)
         stacked.append(jnp.concatenate([w_l, zero], 1))
         stacked.append(jnp.concatenate([zero, w_l], 1))
+    bias = jnp.concatenate([b_in[...]] * 2, 1)
+    coarse = bias.astype(BF16).astype(F32)
+    row16 = lax.broadcasted_iota(I32, (16, 2 * hid), 0)
+    stacked.append(
+        jnp.where(row16 == 0, rows_of(coarse, 16), jnp.where(row16 == 1, rows_of(bias - coarse, 16), 0.0))
+    )
     w1[...] = jnp.concatenate(stacked, 0).T.astype(BF16)
     w2[...] = (0.5 * w_out[...].astype(F32)).astype(BF16)
 
@@ -217,30 +232,35 @@
             )
         add_part(0, g)
 
-    def send_grid(n):
+    def store_grid(n):
         for s in range(n * SPLIT, (n + 1) * SPLIT):
             cols = slice((s - n * SPLIT) * send_cols, (s - n * SPLIT + 1) * send_cols)
             grid[s] = acc[:, cols].reshape(nb, LAT, send_cols).astype(BF16)
             pltpu.make_async_copy(grid.at[s, me], r2.at[s, me], recv2.at[s]).start()
 
-            @pl.loop(1, nb)
-            def _(i):
-                to = peer(i)
-                pltpu.make_async_remote_copy(
-                    src_ref=grid.at[s, to], dst_ref=r2.at[s, me],
-                    send_sem=send2.at[s], recv_sem=recv2.at[s],
-                    device_id={"band": to}, device_id_type=MESH,
-                ).start()
-
-    send_grid(0)
-    for n in range(1, PARTS):
-        acc[...] = clear
-
-        @pl.loop(0, groups)
+    def send_grid(s, i):
+        to = peer(i)
+        pltpu.make_async_remote_copy(
+            src_ref=grid.at[s, to], dst_ref=r2.at[s, me],
+            send_sem=send2.at[s], recv_sem=recv2.at[s],
+            device_id={"band": to}, device_id_type=MESH,
+        ).start()
+
+    steps = groups // SPLIT
+    each = nb // steps
+
+    def scatter(n, split):
+        s = (n - 1) * SPLIT + split
+
+        @pl.loop(0, steps)
         def _(g):
-            add_part(n, g)
-
-        send_grid(n)
+            @pl.when(g > 0)
+            def _():
+                send_grid(s, g * each)
+
+            for k in range(1, each):
+                send_grid(s, g * each + k)
+            add_part(n, split * steps + g)
 
     def transform(n):
         pltpu.make_async_copy(grid.at[n], r2.at[n], recv2.at[n]).wait()
@@ -279,65 +299,98 @@
 
     def encode(p):
         first = pl.multiple_of(p * 2 * CH, 2 * CH)
-        feats = spec[:, pl.ds(first, 2 * CH), :]
-        modes = feats.shape[2]
-        wide = feats.astype(F32)
-        square = jnp.sum(wide * wide, axis=0)
-        pre[...] = jnp.dot(
-            w1[...], feats.reshape(ny * 2 * CH, modes), preferred_element_type=F32
-        )
-        for par in range(2):
-            mean = jnp.sum(square[par * CH : (par + 1) * CH], axis=0, keepdims=True)
-            norm = rows_of(lax.rsqrt(mean * (1.0 / (ny * CH)) + EPS), ROWS)
-            act = []
-            for r in range(0, hid, ROWS):
-                bias = jnp.concatenate([bias1[r : r + ROWS, :]] * (modes // CAP), 1)
-                z = pre[par * hid + r : par * hid + r + ROWS, :] * norm + bias
-                bend = jnp.tanh(z * (0.7978845608028654 + 0.035677408136300125 * (z * z)))
-                act.append((z + z * bend).astype(BF16))
-            stage[:, 2 * p + par, :] = (
-                jnp.dot(w2[...], jnp.concatenate(act), preferred_element_type=F32) + bias2[...]
+        span = spec.shape[2] // STRIPS
+        for strip in range(STRIPS):
+            cols = slice(strip * span, (strip + 1) * span)
+            wide = spec[:, pl.ds(first, 2 * CH), cols].astype(F32)
+            square = jnp.sum(wide * wide, axis=0)
+            norms = []
+            for par in range(2):
+                mean = jnp.sum(square[par * CH : (par + 1) * CH], axis=0, keepdims=True)
+                norms.append(rows_of(lax.rsqrt(mean * (1.0 / (ny * CH)) + EPS), CH))
+            scale = jnp.concatenate(norms, 0)
+            normed = [(wide[l] * scale).astype(BF16) for l in range(ny)]
+            normed.append(jnp.ones((16, span), BF16))
+            pre[strip] = jnp.dot(
+                w1[...], jnp.concatenate(normed, 0), preferred_element_type=F32
             )
+        for strip in range(STRIPS):
+            cols = slice(strip * span, (strip + 1) * span)
+            for par in range(2):
+                act = []
+                for r in range(0, hid, ROWS):
+                    z = pre[strip, par * hid + r : par * hid + r + ROWS, :]
+                    bend = jnp.tanh(z * (0.7978845608028654 + 0.035677408136300125 * (z * z)))
+                    act.append((z + z * bend).astype(BF16))
+                stage[:, 2 * p + par, cols] = (
+                    jnp.dot(w2[...], jnp.concatenate(act), preferred_element_type=F32) + bias2[...]
+                )
 
     ready = [(i + 1) * rows // (2 * CH) for i in range(PIECES)]
 
-    def encode_piece(i):
-        if i % 2 == 0:
-            arrived(right, i, recv_r)
-        else:
-            arrived(left, i, recv_l)
-        arrived(opp, i, recv_o)
-        before = ready[i - 1] if i else 0
-
-        @pl.loop(before, ready[i])
+    def encode_pieces(first, last):
+        for i in range(first, last):
+            if i % 2 == 0:
+                arrived(right, i, recv_r)
+            else:
+                arrived(left, i, recv_l)
+            arrived(opp, i, recv_o)
+        before, after = ready[first - 1] if first else 0, ready[last - 1]
+
+        @pl.loop(before, after)
         def _(p):
             encode(p)
 
-        lo_m, hi_m = before * 2 // 8 * 8, ready[i] * 2 // 8 * 8
+        lo_m, hi_m = before * 2 // 8 * 8, after * 2 // 8 * 8
         if hi_m > lo_m:
             out[:, lo_m:hi_m, :] = stage[:, lo_m:hi_m, :].astype(BF16)
 
-    for n in range(PARTS * SPLIT):
+    def launch(n):
         transform(n)
         own(2 * n)
         own(2 * n + 1)
-        if n in (1, 2, 3):
-            relay(2 * n - 2)
-            relay(2 * n - 1)
-    encode_piece(0)
-    encode_piece(1)
+
+    store_grid(0)
+    acc[...] = clear
+    scatter(1, 0)
+    scatter(1, 1)
+    store_grid(1)
+    acc[...] = clear
+    scatter(2, 0)
+    launch(0)
+    scatter(2, 1)
+    launch(1)
+    store_grid(2)
+
+    @pl.loop(1, nb)
+    def _(i):
+        send_grid(2 * SPLIT, i)
+
+    relay(0)
+    relay(1)
+
+    @pl.loop(1, nb)
+    def _(i):
+        send_grid(2 * SPLIT + 1, i)
+
+    launch(2)
+    launch(3)
+    for i in range(2, 6):
+        relay(i)
+    launch(4)
     relay(6)
     relay(7)
-    encode_piece(2)
-    encode_piece(3)
+    launch(5)
+    encode_pieces(0, 2)
+    encode_pieces(2, 4)
     relay(8)
     relay(9)
-    for i in range(4, 8):
-        encode_piece(i)
+    encode_pieces(4, 6)
     relay(10)
     relay(11)
-    for i in range(8, PIECES):
-        encode_piece(i)
+    encode_pieces(6, 8)
+    encode_pieces(8, 10)
+    encode_pieces(10, 12)
 
     pltpu.make_async_copy(s1.at[pl.ds(0, nb - 1)], r1.at[pl.ds(0, nb - 1)], send1).wait()
     for h in range(PARTS * SPLIT):
@@ -377,7 +430,6 @@
         scratch_shapes=[
             *(pltpu.VMEM(arg.shape, arg.dtype) for arg in args),
             pltpu.VMEM((nb, 1), F32),
-            pltpu.VMEM((w_in.shape[1], CAP), F32),
             pltpu.VMEM((outs, 1), F32),
             pltpu.VMEM((obs // LANES * AUX, LANES), BF16),
             pltpu.VMEM((nb, AUX, CAP), BF16),
@@ -387,9 +439,9 @@
             pltpu.VMEM((PARTS * SPLIT, nb, LAT, send_cols), BF16),
             pltpu.VMEM((PARTS * SPLIT, nb, LAT, send_cols), BF16),
             pltpu.VMEM((ny, LON * CH, modes), BF16),
-            pltpu.VMEM((2 * w_in.shape[1], 2 * w_in.shape[0]), BF16),
+            pltpu.VMEM((2 * w_in.shape[1], 2 * w_in.shape[0] + 16), BF16),
             pltpu.VMEM((outs, w_out.shape[0]), BF16),
-            pltpu.VMEM((2 * w_in.shape[1], modes), F32),
+            pltpu.VMEM((STRIPS, 2 * w_in.shape[1], modes // STRIPS), F32),
             pltpu.VMEM((outs, LON, modes), F32),
             dma((INPUTS,)), dma, dma((groups,)), dma((PARTS * SPLIT,)), dma((PARTS * SPLIT,)),
             dma, dma((PIECES,)), dma((PIECES,)), dma((PIECES,)),

time: 76.1 us -> 67.9 us (0.89)
  Pallas kernels: 74 us -> 66.1 us
    pallas_call x1, Pallas kernels: 74 us -> 66.1 us  [on_device(): pl.pallas_call(functools.partial(kernel, nb, ny), out_shape=jax.ShapeDtyp...]
where the time goes in v3:
time: 67.9 us; the launch traced here: 67.4 us
  Pallas kernels  66.1 us (97%)
  local copies, waits for them, and re-layouts  1.32 us (2%)
    pallas_call x1, Pallas kernels, on_device(): pl.pallas_call(functools.partial(kernel, nb, ny), out_shape=jax.ShapeDtyp...  66.1 us

profile of v3, /device:TPU:32, one launch (start us, length us, event | category | flops | bytes accessed | tf_op | source)
XLA Modules:
  0.0 67.4 jit_solution(9947477957867985518)
XLA Ops:
  0.0 66.1 %shard_map.109 = bf16[64,32,512]{2,1,0:T(8,128)(2,1)S(1)} custom-call(bf16[24,4096]{1,0:T(8,128)(2,1)} %bitcast.7, bf16[32,128]{1,0:T(8,128)(2,1)} %bitcast.11, s32[32,128]{1,0:T(8,128)} %bitcast.10, s32[64,128]{1,0:T(8,128)} %bitcast.8, s32[1,64]{1,0:T(1,128)} %refs_4_.1, f32[8,8]{1,0:T(8,128)} %constant.4.clone.refs_5_, bf16[512,512]{1,0:T(8,128)(2,1)} %constant.9.refs_6_, ...), custom_call_target="tpu_custom_call" | custom-call | tf_op jit(solution)/shard_map/pallas_call | solution.py:425
  66.1 1.3 %copy.13 = bf16[64,32,512]{2,1,0:T(8,128)(2,1)} copy(bf16[64,32,512]{2,1,0:T(8,128)(2,1)S(1)} %shard_map.109) | data formatting | bytes 4194304

commit v4 on v3

--- a/solution.py
+++ b/solution.py
@@ -17,7 +17,7 @@
 LANES = 256
 INPUTS = 11
 GROUP = 8
-STRIDE = 27
+DEPTHS, CORES = 8, 2
 PARTS = 3
 SPLIT = 2
 DEPTH = 8
@@ -67,17 +67,43 @@
     groups = nb // GROUP
     hid = b_in.shape[1]
 
-    def peer(i):
-        return lax.rem(me + i * STRIDE, nb)
+    wide_x = nb // (DEPTHS * CORES)
+    my_x, my_z, my_core = me // (DEPTHS * CORES), lax.rem(me // CORES, DEPTHS), lax.rem(me, CORES)
+
+    def far_first(j, size):
+        return size // 2 + (j + 1) // 2 * (1 - 2 * (j % 2))
+
+    in_plane = [
+        lax.rem(my_x + far_first(j // CORES, wide_x), wide_x) * (DEPTHS * CORES)
+        + lax.rem(my_core + CORES - 1 - j % CORES, CORES)
+        for j in range(GROUP)
+    ]
+
+    def along_z(k):
+        step = DEPTHS // 2 + (k + 1) // 2 * (1 - 2 * lax.rem(k, 2))
+        return lax.rem(my_z + step, DEPTHS) * CORES
+
+    def unless_own(j, other, do):
+        if j < GROUP - 1:
+            do()
+        else:
+            pl.when(other)(do)
 
     loads = [pltpu.make_async_copy(hbm[k], local[k], load.at[k]) for k in range(INPUTS)]
     for copy in loads:
         copy.start()
     barrier = pltpu.get_barrier_semaphore()
 
-    @pl.loop(1, nb)
-    def _(i):
-        pl.semaphore_signal(barrier, inc=1, device_id={"band": peer(i)}, device_id_type=MESH)
+    @pl.loop(0, groups)
+    def _(k):
+        z = along_z(k)
+        for j in range(GROUP):
+            unless_own(
+                j, k < groups - 1,
+                lambda j=j: pl.semaphore_signal(
+                    barrier, inc=1, device_id={"band": in_plane[j] + z}, device_id_type=MESH
+                ),
+            )
 
     for y in (left, right):
         pl.semaphore_signal(barrier, inc=1, device_id={"lev": y}, device_id_type=MESH)
@@ -111,10 +137,10 @@
     lane = lax.broadcasted_iota(I32, (1, CAP), 1)
     sub = lax.broadcasted_iota(I32, (LANES, CAP), 0)
 
-    def sort_batch(step):
+    def sort_batch(k, first):
         hots, his = [], []
-        for u in range(batch):
-            b = peer(step * batch + u)
+        for j in range(first, first + batch):
+            b = in_plane[j] + along_z(k)
             idx = bl[pl.ds(b, 1), :]
             live = lane.astype(F32) < live_n[pl.ds(b, 1), :]
             his.append(jnp.where(live, idx // LANES, -1))
@@ -126,33 +152,42 @@
             block = jnp.where(hi == h, picked[h * AUX : (h + 1) * AUX], block)
         block = block.astype(BF16)
         for u in range(batch):
-            s1[step * batch + u] = block[:, u * CAP : (u + 1) * CAP]
-
-    def send_block(i):
-        pltpu.make_async_remote_copy(
-            src_ref=s1.at[i], dst_ref=r1.at[i],
-            send_sem=send1, recv_sem=recv1.at[i // GROUP],
-            device_id={"band": peer(i)}, device_id_type=MESH,
-        ).start()
-
-    early = nb // batch * 3 // 4
+            s1[k * GROUP + first + u] = block[:, u * CAP : (u + 1) * CAP]
+
+    def send_block(k, j):
+        i = k * GROUP + j
+
+        def go():
+            pltpu.make_async_remote_copy(
+                src_ref=s1.at[i], dst_ref=r1.at[i],
+                send_sem=send1, recv_sem=recv1.at[k],
+                device_id={"band": in_plane[j] + along_z(k)}, device_id_type=MESH,
+            ).start()
+
+        unless_own(j, k < groups - 1, go)
+
+    early = groups * 3 // 4
 
     @pl.loop(0, early)
-    def _(step):
-        sort_batch(step)
+    def _(k):
+        for first in range(0, GROUP, batch):
+            sort_batch(k, first)
 
     pl.semaphore_wait(barrier, nb - 1 + 2)
-    pltpu.make_async_copy(s1.at[0], r1.at[0], recv1.at[0]).start()
-
-    @pl.loop(1, early * batch)
-    def _(i):
-        send_block(i)
-
-    @pl.loop(early, nb // batch)
-    def _(step):
-        sort_batch(step)
-        for u in range(batch):
-            send_block(step * batch + u)
+
+    @pl.loop(0, early)
+    def _(k):
+        for j in range(GROUP):
+            send_block(k, j)
+
+    @pl.loop(early, groups)
+    def _(k):
+        for first in range(0, GROUP, batch):
+            sort_batch(k, first)
+            for j in range(first, first + batch):
+                send_block(k, j)
+
+    pltpu.make_async_copy(s1.at[nb - 1], r1.at[nb - 1], recv1.at[groups - 1]).start()
 
     zero = jnp.zeros((CH, hid), F32)
     stacked = []
@@ -213,7 +248,8 @@
     acc[...] = clear
 
     @pl.loop(0, groups)
-    def _(g):
+    def _(turn):
+        g = lax.rem(turn + groups - 1, groups)
         pltpu.make_async_copy(
             s1.at[pl.ds(0, GROUP)], r1.at[pl.ds(0, GROUP)], recv1.at[g]
         ).wait()
@@ -238,28 +274,28 @@
             grid[s] = acc[:, cols].reshape(nb, LAT, send_cols).astype(BF16)
             pltpu.make_async_copy(grid.at[s, me], r2.at[s, me], recv2.at[s]).start()
 
-    def send_grid(s, i):
-        to = peer(i)
-        pltpu.make_async_remote_copy(
-            src_ref=grid.at[s, to], dst_ref=r2.at[s, me],
-            send_sem=send2.at[s], recv_sem=recv2.at[s],
-            device_id={"band": to}, device_id_type=MESH,
-        ).start()
+    def send_grid(s, k):
+        z = along_z(k)
+        for j in range(GROUP):
+
+            def go(to=in_plane[j] + z):
+                pltpu.make_async_remote_copy(
+                    src_ref=grid.at[s, to], dst_ref=r2.at[s, me],
+                    send_sem=send2.at[s], recv_sem=recv2.at[s],
+                    device_id={"band": to}, device_id_type=MESH,
+                ).start()
+
+            unless_own(j, k < groups - 1, go)
 
     steps = groups // SPLIT
-    each = nb // steps
-
-    def scatter(n, split):
+
+    def scatter(n, split, first, last):
         s = (n - 1) * SPLIT + split
 
-        @pl.loop(0, steps)
+        @pl.loop(first, last)
         def _(g):
-            @pl.when(g > 0)
-            def _():
-                send_grid(s, g * each)
-
-            for k in range(1, each):
-                send_grid(s, g * each + k)
+            for k in range(SPLIT):
+                send_grid(s, g * SPLIT + k)
             add_part(n, split * steps + g)
 
     def transform(n):
@@ -284,10 +320,6 @@
 
     def arrived(level, i, sem):
         pltpu.make_async_copy(piece(level, i), piece(level, i), sem.at[i]).wait()
-
-    def own(i):
-        push(lev, i, right, recv_l)
-        push(lev, i, left, recv_r)
 
     def relay(i):
         if i % 2 == 0:
@@ -347,31 +379,35 @@
 
     def launch(n):
         transform(n)
-        own(2 * n)
-        own(2 * n + 1)
+        push(lev, 2 * n, right, recv_l)
+        push(lev, 2 * n + 1, left, recv_r)
+        push(lev, 2 * n, left, recv_r)
+        push(lev, 2 * n + 1, right, recv_l)
 
     store_grid(0)
     acc[...] = clear
-    scatter(1, 0)
-    scatter(1, 1)
+    scatter(1, 0, 0, steps)
+    scatter(1, 1, 0, steps)
     store_grid(1)
     acc[...] = clear
-    scatter(2, 0)
+    scatter(2, 0, 0, steps // 2)
     launch(0)
-    scatter(2, 1)
+    scatter(2, 0, steps // 2, steps)
+    scatter(2, 1, 0, steps // 2)
     launch(1)
+    scatter(2, 1, steps // 2, steps)
     store_grid(2)
 
-    @pl.loop(1, nb)
-    def _(i):
-        send_grid(2 * SPLIT, i)
+    @pl.loop(0, groups)
+    def _(k):
+        send_grid(2 * SPLIT, k)
 
     relay(0)
     relay(1)
 
-    @pl.loop(1, nb)
-    def _(i):
-        send_grid(2 * SPLIT + 1, i)
+    @pl.loop(0, groups)
+    def _(k):
+        send_grid(2 * SPLIT + 1, k)
 
     launch(2)
     launch(3)

time: 67.9 us -> 66.3 us (0.976)
  Pallas kernels: 66.1 us -> 64.7 us
    pallas_call x1, Pallas kernels: 66.1 us -> 64.7 us  [on_device(): pl.pallas_call(functools.partial(kernel, nb, ny), out_shape=jax.ShapeDtyp...]
where the time goes in v4:
time: 66.3 us; the launch traced here: 66 us
  Pallas kernels  64.7 us (98%)
  local copies, waits for them, and re-layouts  1.32 us (2%)
    pallas_call x1, Pallas kernels, on_device(): pl.pallas_call(functools.partial(kernel, nb, ny), out_shape=jax.ShapeDtyp...  64.7 us

profile of v4, /device:TPU:32, one launch (start us, length us, event | category | flops | bytes accessed | tf_op | source)
XLA Modules:
  0.0 66.0 jit_solution(268898811231108553)
XLA Ops:
  0.0 64.7 %shard_map.109 = bf16[64,32,512]{2,1,0:T(8,128)(2,1)S(1)} custom-call(bf16[24,4096]{1,0:T(8,128)(2,1)} %bitcast.7, bf16[32,128]{1,0:T(8,128)(2,1)} %bitcast.11, s32[32,128]{1,0:T(8,128)} %bitcast.10, s32[64,128]{1,0:T(8,128)} %bitcast.8, s32[1,64]{1,0:T(1,128)} %refs_4_.1, f32[8,8]{1,0:T(8,128)} %constant.4.clone.refs_5_, bf16[512,512]{1,0:T(8,128)(2,1)} %constant.9.refs_6_, ...), custom_call_target="tpu_custom_call" | custom-call | tf_op jit(solution)/shard_map/pallas_call | solution.py:461
  64.7 1.3 %copy.13 = bf16[64,32,512]{2,1,0:T(8,128)(2,1)} copy(bf16[64,32,512]{2,1,0:T(8,128)(2,1)S(1)} %shard_map.109) | data formatting | bytes 4194304

commit v5 on v4

--- a/solution.py
+++ b/solution.py
@@ -166,7 +166,7 @@
 
         unless_own(j, k < groups - 1, go)
 
-    early = groups * 3 // 4
+    early = groups // 2
 
     @pl.loop(0, early)
     def _(k):
@@ -422,9 +422,9 @@
     relay(8)
     relay(9)
     encode_pieces(4, 6)
+    encode_pieces(6, 8)
     relay(10)
     relay(11)
-    encode_pieces(6, 8)
     encode_pieces(8, 10)
     encode_pieces(10, 12)
 

time: 66.3 us -> 66.2 us (level)
  no operation moved by 1% of the time
where the time goes in v5:
time: 66.2 us; the launch traced here: 66 us
  Pallas kernels  64.6 us (98%)
  local copies, waits for them, and re-layouts  1.32 us (2%)
    pallas_call x1, Pallas kernels, on_device(): pl.pallas_call(functools.partial(kernel, nb, ny), out_shape=jax.ShapeDtyp...  64.6 us

profile of v5, /device:TPU:32, one launch (start us, length us, event | category | flops | bytes accessed | tf_op | source)
XLA Modules:
  0.0 66.0 jit_solution(16657720407977176416)
XLA Ops:
  0.0 64.6 %shard_map.109 = bf16[64,32,512]{2,1,0:T(8,128)(2,1)S(1)} custom-call(bf16[24,4096]{1,0:T(8,128)(2,1)} %bitcast.7, bf16[32,128]{1,0:T(8,128)(2,1)} %bitcast.11, s32[32,128]{1,0:T(8,128)} %bitcast.10, s32[64,128]{1,0:T(8,128)} %bitcast.8, s32[1,64]{1,0:T(1,128)} %refs_4_.1, f32[8,8]{1,0:T(8,128)} %constant.4.clone.refs_5_, bf16[512,512]{1,0:T(8,128)(2,1)} %constant.9.refs_6_, ...), custom_call_target="tpu_custom_call" | custom-call | tf_op jit(solution)/shard_map/pallas_call | solution.py:461
  64.6 1.3 %copy.13 = bf16[64,32,512]{2,1,0:T(8,128)(2,1)} copy(bf16[64,32,512]{2,1,0:T(8,128)(2,1)S(1)} %shard_map.109) | data formatting | bytes 4194304
